TPU v7x, 32 devices: a whole 2x2x4 slice. The times are simulated.
32 devices in a mesh: vec: 8 (over z, core), rep: 4 (over y, x).
Axes of the slice: x: 2, y: 2, z: 4, core: 2. Of those that a mesh axis runs over, the one named last changes fastest.
Arguments:
- vectors: bfloat16 [1024, 1024], P('vec'), may hold values from 0 to 2
- pivot_index: int32 [4, 8], P('rep'), may hold values from 0 to 1023
Outputs:
- similarity: bfloat16 [7, 32, 1024, 128], P(None, 'rep', 'vec')
All inputs are finite; a program needn't handle non-finite values.
Results may differ from a plain program's by a relative error of at most 0.011.
Values may be sent and summed in bfloat16 or wider, within the bound.
A program may use at most 64 MiB of HBM per device.

v0:
```python
import math
import jax
import jax.numpy as jnp
from jax import lax
from jax.sharding import PartitionSpec as P

HALF = 3


def from_behind(block, axis, distance):
    devices = range(lax.axis_size(axis))
    route = [((i - distance) % len(devices), i) for i in devices]
    return lax.ppermute(block, axis, route)


def contract(left, right):
    return lax.dot_general(
        left, right, (((1,), (1,)), ((), ())), preferred_element_type=jnp.float32
    )


def on_device(vectors, pivot_index):
    block_rows, fields = vectors.shape
    position = lax.axis_index("vec")
    wanted = pivot_index.reshape(-1) - position * block_rows
    columns = jnp.arange(block_rows, dtype=jnp.int32)
    onehot = (wanted[:, None] == columns[None, :]).astype(jnp.bfloat16)
    local_rows = jnp.dot(onehot, vectors, preferred_element_type=jnp.float32)
    pivots = lax.psum(local_rows, "vec")
    count = pivots.shape[0]
    centre = jnp.sum(pivots, axis=1) / fields
    scaled = (vectors.astype(jnp.float32)[None, :, :] * pivots[:, None, :]).astype(jnp.bfloat16)
    scaled = scaled.reshape(count * block_rows, fields)
    replicas = lax.axis_size("rep")
    share = block_rows // replicas
    own_rows = lax.dynamic_slice_in_dim(vectors, lax.axis_index("rep") * share, share, 0)
    window = 2 * HALF + 1
    triples = [None] * window
    grams = [None] * window
    triples[HALF] = contract(scaled, vectors)
    grams[HALF] = contract(own_rows, vectors)
    lower = vectors
    upper = vectors
    for reach in range(1, HALF + 1):
        lower = from_behind(lower, "vec", 1)
        upper = from_behind(upper, "vec", -1)
        triples[HALF - reach] = contract(scaled, lower)
        grams[HALF - reach] = contract(own_rows, lower)
        triples[HALF + reach] = contract(scaled, upper)
        grams[HALF + reach] = contract(own_rows, upper)
    triple_all = jnp.stack(triples).reshape(window, count, block_rows, block_rows)
    gram_all = jnp.stack(grams)
    gram_all = lax.all_gather(gram_all, "rep", axis=1, tiled=True)
    similarity = (triple_all - centre[None, :, None, None] * gram_all[:, None, :, :]) / math.sqrt(
        fields
    )
    return similarity.astype(jnp.bfloat16)


def solution(mesh):
    in_specs = (P("vec", None), P("rep", None))
    out_specs = P(None, "rep", "vec", None)
    return jax.shard_map(
        on_device, mesh=mesh, in_specs=in_specs, out_specs=out_specs, check_vma=False
    )
```

profile of v0, /device:TPU:0, one launch (start us, length us, event | category | flops | bytes accessed | tf_op | source)
XLA Modules:
  0.0 71.4 jit_solution(5123657337619987184)
XLA Ops:
  0.0 0.5 collective-permute-start
  0.5 4.0 %collective-permute-start.3 = (bf16[128,1024]{1,0:T(8,128)(2,1)}, bf16[128,1024]{1,0:T(8,128)(2,1)S(1)}, u32[]{:S(2)}, u32[]{:S(2)}) collective-permute-start(bf16[128,1024]{1,0:T(8,128)(2,1)} %param.2), channel_id=1, source_target_pairs={{4,0},{8,4},{12,8},{16,12},{20,16},{24,20},{28,24},{0,28},{5,1},{9... | collective-permute-start | bytes 786440 | tf_op jit(solution)/shard_map/ppermute | solution.py:13
  4.5 4.5 %collective-permute-done = bf16[128,1024]{1,0:T(8,128)(2,1)S(1)} collective-permute-done((bf16[128,1024]{1,0:T(8,128)(2,1)}, bf16[128,1024]{1,0:T(8,128)(2,1)S(1)}, u32[]{:S(2)}, u32[]{:S(2)}) %collective-permute-start) | collective-permute-done | bytes 262176 | tf_op jit(solution)/shard_map/ppermute | solution.py:13
  9.0 0.0 collective-permute-start.1
  9.0 0.7 subtract_bitcast_fusion
  9.7 0.0 collective-permute-done.3
  9.7 3.5 %collective-permute-start.4 = (bf16[128,1024]{1,0:T(8,128)(2,1)S(1)}, bf16[128,1024]{1,0:T(8,128)(2,1)S(1)}, u32[]{:S(2)}, u32[]{:S(2)}) collective-permute-start(bf16[128,1024]{1,0:T(8,128)(2,1)S(1)} %collective-permute-done.3), channel_id=1, source_target_pairs={{4,0},{8,4},{12,8},{16,12},{20,16},{24,20},{28,24},{0,28},{5,1},{9... | collective-permute-start | bytes 786440 | tf_op jit(solution)/shard_map/ppermute | solution.py:13
  13.2 3.5 %collective-permute-done.1 = bf16[128,1024]{1,0:T(8,128)(2,1)S(1)} collective-permute-done((bf16[128,1024]{1,0:T(8,128)(2,1)S(1)}, bf16[128,1024]{1,0:T(8,128)(2,1)S(1)}, u32[]{:S(2)}, u32[]{:S(2)}) %collective-permute-start.1) | collective-permute-done | bytes 262176 | tf_op jit(solution)/shard_map/ppermute | solution.py:13
  16.7 0.0 collective-permute-start.2
  16.7 1.1 %fusion.56 = f32[8,1024]{1,0:T(8,128)S(1)} fusion(bf16[128,1024]{1,0:T(8,128)(2,1)} %param.2, s32[8]{0:T(128)S(1)} %subtract_bitcast_fusion), kind=kOutput, calls=%fused_computation.66 | convolution fusion | flops 2098176 | bytes 294944 | tf_op jit(solution)/shard_map/dot_general | solution.py:28
  17.8 1.0 %convert_element_type.21 = f32[128,1024]{1,0:T(8,128)S(1)} convert(bf16[128,1024]{1,0:T(8,128)(2,1)} %param.2) | non-fusion elementwise | flops 131072 | bytes 786432 | tf_op jit(solution)/shard_map/convert_element_type | solution.py:32
  18.8 29.4 %psum.7 = f32[8,1024]{1,0:T(8,128)S(1)} all-reduce(f32[8,1024]{1,0:T(8,128)S(1)} %fusion.56), channel_id=1, replica_groups=mesh['vec'=8,'rep'=4] {'vec'}, use_global_device_ids=true, to_apply=%region_0.0 | all-reduce | flops 8192 | bytes 65536 | tf_op jit(solution)/shard_map/psum | solution.py:29
  48.3 0.1 reduce_sum.9
  48.4 0.0 collective-permute-done.4
  48.4 0.1 collective-permute-start.5
  48.5 0.0 collective-permute-done.2
  48.5 1.0 %fusion.41 = f32[7,32,128]{2,1,0:T(8,128)S(1)} fusion(bf16[128,1024]{1,0:T(8,128)(2,1)S(1)} %collective-permute-done.2, bf16[128,1024]{1,0:T(8,128)(2,1)} %param.2, s32[]{:T(128)S(6)} %select_n.3), kind=kOutput, calls=%fused_computation.50 | convolution fusion | flops 8388607 | bytes 344068 | tf_op jit(solution)/shard_map/dot_general | solution.py:17
  49.5 1.0 %fusion.40 = f32[7,32,128]{2,1,0:T(8,128)S(1)} fusion(f32[7,32,128]{2,1,0:T(8,128)S(1)} %fusion.41, bf16[128,1024]{1,0:T(8,128)(2,1)S(1)} %collective-permute-done.1, bf16[128,1024]{1,0:T(8,128)(2,1)} %param.2, s32[]{:T(128)S(6)} %select_n.3), kind=kOutput, calls=%fused_computation.48 | convolution fusion | flops 8388608 | bytes 344068 | tf_op jit(solution)/shard_map/dot_general | solution.py:17
  50.5 1.0 %fusion.39 = f32[7,32,128]{2,1,0:T(8,128)S(1)} fusion(f32[7,32,128]{2,1,0:T(8,128)S(1)} %fusion.40, bf16[128,1024]{1,0:T(8,128)(2,1)S(1)} %collective-permute-done, bf16[128,1024]{1,0:T(8,128)(2,1)} %param.2, s32[]{:T(128)S(6)} %select_n.3), kind=kOutput, calls=%fused_computation.46 | convolution fusion | flops 8388608 | bytes 344068 | tf_op jit(solution)/shard_map/dot_general | solution.py:17
  51.6 1.2 %fusion.38 = f32[7,32,128]{2,1,0:T(8,128)S(1)} fusion(f32[7,32,128]{2,1,0:T(8,128)S(1)} %fusion.39, bf16[128,1024]{1,0:T(8,128)(2,1)} %param.2, s32[]{:T(128)S(6)} %select_n.3), kind=kOutput, calls=%fused_computation.44 | convolution fusion | flops 8388608 | bytes 344068 | tf_op jit(solution)/shard_map/dot_general | solution.py:17
  52.8 0.0 copy-start
  52.8 0.7 %fusion.22 = f32[7,8,128,128]{3,2,1,0:T(8,128)S(1)} fusion(f32[8,1024]{1,0:T(8,128)S(1)} %psum.7, f32[128,1024]{1,0:T(8,128)S(1)} %convert_element_type.21, bf16[128,1024]{1,0:T(8,128)(2,1)S(1)} %collective-permute-done.2), kind=kOutput, calls=%fused_computation.24 | convolution fusion | flops 270532608 | bytes 1343488 | tf_op jit(solution)/shard_map/dot_general | solution.py:17
  53.6 0.7 fusion.24
  54.3 0.7 fusion.26
  55.0 0.0 copy-done
  55.0 0.2 fusion.37
  55.2 0.2 fusion.36
  55.4 0.7 %fusion.28 = f32[7,8,128,128]{3,2,1,0:T(8,128)S(1)} fusion(f32[7,8,128,128]{3,2,1,0:T(8,128)S(1)} %fusion.26, f32[8,1024]{1,0:T(8,128)S(1)} %psum.7, f32[128,1024]{1,0:T(8,128)S(1)} %convert_element_type.21, bf16[128,1024]{1,0:T(8,128)(2,1)S(1)} %copy-done), kind=kOutput, calls=%fused_computation.30 | convolution fusion | flops 270532608 | bytes 1343488 | tf_op jit(solution)/shard_map/dot_general | solution.py:17
  56.1 0.0 collective-permute-done.5
  56.1 0.2 fusion.35
  56.3 11.0 %all_gather.3 = f32[7,128,128]{2,1,0:T(8,128)S(1)} all-gather(f32[7,32,128]{2,1,0:T(8,128)S(1)} %fusion.35), channel_id=1, replica_groups=mesh['vec'=8,'rep'=4] {'rep'}, dimensions={1}, use_global_device_ids=true | all-gather | bytes 573440 | tf_op jit(solution)/shard_map/all_gather | solution.py:53
  67.3 0.7 fusion.30
  68.0 0.7 fusion.32
  68.8 0.7 fusion.34
  69.5 1.9 %multiply_convert_fusion.8 = bf16[7,8,128,128]{3,2,1,0:T(8,128)(2,1)} fusion(f32[7,8,128,128]{3,2,1,0:T(8,128)S(1)} %fusion.34, f32[7,128,128]{2,1,0:T(8,128)S(1)} %all_gather.3, f32[8]{0:T(128)S(1)} %broadcast_multiply_fusion), kind=kLoop, calls=%fused_computation.8 | loop fusion | flops 3670016 | bytes 5963808 | tf_op jit(solution)/shard_map/convert_element_type | solution.py:57
  (1 shorter events, 0.0 us)
Async XLA Ops:
  0.0 9.0 %collective-permute-start = (bf16[128,1024]{1,0:T(8,128)(2,1)}, bf16[128,1024]{1,0:T(8,128)(2,1)S(1)}, u32[]{:S(2)}, u32[]{:S(2)}) collective-permute-start(bf16[128,1024]{1,0:T(8,128)(2,1)} %param.2), channel_id=1, source_target_pairs={{28,0},{0,4},{4,8},{8,12},{12,16},{16,20},{20,24},{24,28},{29,1},{... | collective-permute-start | bytes 786440 | tf_op jit(solution)/shard_map/ppermute | solution.py:13
  0.5 9.2 %collective-permute-start.3 = (bf16[128,1024]{1,0:T(8,128)(2,1)}, bf16[128,1024]{1,0:T(8,128)(2,1)S(1)}, u32[]{:S(2)}, u32[]{:S(2)}) collective-permute-start(bf16[128,1024]{1,0:T(8,128)(2,1)} %param.2), channel_id=1, source_target_pairs={{4,0},{8,4},{12,8},{16,12},{20,16},{24,20},{28,24},{0,28},{5,1},{9... | collective-permute-start | bytes 786440 | tf_op jit(solution)/shard_map/ppermute | solution.py:13
  9.0 7.7 %collective-permute-start.1 = (bf16[128,1024]{1,0:T(8,128)(2,1)S(1)}, bf16[128,1024]{1,0:T(8,128)(2,1)S(1)}, u32[]{:S(2)}, u32[]{:S(2)}) collective-permute-start(bf16[128,1024]{1,0:T(8,128)(2,1)S(1)} %collective-permute-done), channel_id=1, source_target_pairs={{28,0},{0,4},{4,8},{8,12},{12,16},{16,20},{20,24},{24,28},{29,1},{... | collective-permute-start | bytes 786440 | tf_op jit(solution)/shard_map/ppermute | solution.py:13
  9.7 38.7 %collective-permute-start.4 = (bf16[128,1024]{1,0:T(8,128)(2,1)S(1)}, bf16[128,1024]{1,0:T(8,128)(2,1)S(1)}, u32[]{:S(2)}, u32[]{:S(2)}) collective-permute-start(bf16[128,1024]{1,0:T(8,128)(2,1)S(1)} %collective-permute-done.3), channel_id=1, source_target_pairs={{4,0},{8,4},{12,8},{16,12},{20,16},{24,20},{28,24},{0,28},{5,1},{9... | collective-permute-start | bytes 786440 | tf_op jit(solution)/shard_map/ppermute | solution.py:13
  16.7 31.8 %collective-permute-start.2 = (bf16[128,1024]{1,0:T(8,128)(2,1)S(1)}, bf16[128,1024]{1,0:T(8,128)(2,1)S(1)}, u32[]{:S(2)}, u32[]{:S(2)}) collective-permute-start(bf16[128,1024]{1,0:T(8,128)(2,1)S(1)} %collective-permute-done.1), channel_id=1, source_target_pairs={{28,0},{0,4},{4,8},{8,12},{12,16},{16,20},{20,24},{24,28},{29,1},{... | collective-permute-start | bytes 786440 | tf_op jit(solution)/shard_map/ppermute | solution.py:13
  48.4 7.7 %collective-permute-start.5 = (bf16[128,1024]{1,0:T(8,128)(2,1)S(1)}, bf16[128,1024]{1,0:T(8,128)(2,1)S(1)}, u32[]{:S(2)}, u32[]{:S(2)}) collective-permute-start(bf16[128,1024]{1,0:T(8,128)(2,1)S(1)} %collective-permute-done.4), channel_id=1, source_target_pairs={{4,0},{8,4},{12,8},{16,12},{20,16},{24,20},{28,24},{0,28},{5,1},{9... | collective-permute-start | bytes 786440 | tf_op jit(solution)/shard_map/ppermute | solution.py:13
  52.8 2.2 %copy-start = (bf16[128,1024]{1,0:T(8,128)(2,1)S(1)}, bf16[128,1024]{1,0:T(8,128)(2,1)}, u32[]{:S(2)}) copy-start(bf16[128,1024]{1,0:T(8,128)(2,1)} %param.2) | copy-start | bytes 786436
where the time goes:
time: 71.7 us; the launch traced here: 71.4 us
  blocking collectives  40.5 us (56%)
  matrix products  11 us (15%)
  starting transfers between devices  8.13 us (11%)
  waiting for transfers between devices  7.96 us (11%)
  other arithmetic  3.69 us (5%)
    psum x1, blocking collectives, on_device(): pivots = lax.psum(local_rows, 'vec')  29.4 us
    all_gather x1, blocking collectives, on_device(): gram_all = lax.all_gather(gram_all, 'rep', axis=1, tiled=True)  11 us
    dot_general x14, matrix products, contract(): lax.dot_general(left, right, (((1,), (1,)), ((), ())), preferred_element_...  9.87 us
    ppermute x6, starting transfers between devices, from_behind(): return lax.ppermute(block, axis, route)  8.13 us
    ppermute x6, waiting for transfers between devices, from_behind(): return lax.ppermute(block, axis, route)  7.96 us
    convert_element_type x1, other arithmetic, on_device(): return similarity.astype(jnp.bfloat16)  1.9 us
  transfers between devices with their start and end apart: 6, of which 2 were waited for; matrix products, arithmetic and copies ran while one was open for 15% of the time, Pallas kernels for 0%

commit v1 on v0

--- a/solution.py
+++ b/solution.py
@@ -26,7 +26,8 @@
     columns = jnp.arange(block_rows, dtype=jnp.int32)
     onehot = (wanted[:, None] == columns[None, :]).astype(jnp.bfloat16)
     local_rows = jnp.dot(onehot, vectors, preferred_element_type=jnp.float32)
-    pivots = lax.psum(local_rows, "vec")
+    parts = lax.all_gather(local_rows, "vec", axis=0, tiled=False)
+    pivots = parts.sum(axis=0)
     count = pivots.shape[0]
     centre = jnp.sum(pivots, axis=1) / fields
     scaled = (vectors.astype(jnp.float32)[None, :, :] * pivots[:, None, :]).astype(jnp.bfloat16)

time: 71.7 us -> 60.8 us (0.85)
  blocking collectives: 40.5 us -> 25.6 us
  starting transfers between devices: 8.13 us -> 11.5 us
  matrix products: 11 us -> 11.8 us
    psum x1 -> x0, blocking collectives: 29.4 us -> none  [on_device(): pivots = lax.psum(local_rows, 'vec')]
    all_gather x0 -> x1, blocking collectives: none -> 15.8 us  [on_device(): parts = lax.all_gather(local_rows, 'vec', axis=0, tiled=False)]
    ppermute x6, starting transfers between devices: 8.13 us -> 11.5 us  [from_behind(): return lax.ppermute(block, axis, route)]
    all_gather x1, blocking collectives: 11 us -> 9.8 us  [on_device(): gram_all = lax.all_gather(gram_all, 'rep', axis=1, tiled=True)]
    dot_general x14, matrix products: 9.87 us -> 10.7 us  [contract(): lax.dot_general(left, right, (((1,), (1,)), ((), ())), preferred_element_...]
  transfers between devices with their start and end apart: 6 -> 6, of which waited for: 2 -> 2; matrix products, arithmetic and copies ran while one was open for 15% -> 14% of each run, Pallas kernels for 0% -> 0%
where the time goes in v1:
time: 60.8 us; the launch traced here: 60.3 us
  blocking collectives  25.6 us (42%)
  matrix products  11.8 us (19%)
  starting transfers between devices  11.5 us (19%)
  waiting for transfers between devices  7.57 us (12%)
  other arithmetic  3.72 us (6%)
    all_gather x1, blocking collectives, on_device(): parts = lax.all_gather(local_rows, 'vec', axis=0, tiled=False)  15.8 us
    ppermute x6, starting transfers between devices, from_behind(): return lax.ppermute(block, axis, route)  11.5 us
    dot_general x14, matrix products, contract(): lax.dot_general(left, right, (((1,), (1,)), ((), ())), preferred_element_...  10.7 us
    all_gather x1, blocking collectives, on_device(): gram_all = lax.all_gather(gram_all, 'rep', axis=1, tiled=True)  9.8 us
    ppermute x6, waiting for transfers between devices, from_behind(): return lax.ppermute(block, axis, route)  7.57 us
    convert_element_type x1, other arithmetic, on_device(): return similarity.astype(jnp.bfloat16)  1.9 us
  transfers between devices with their start and end apart: 6, of which 2 were waited for; matrix products, arithmetic and copies ran while one was open for 14% of the time, Pallas kernels for 0%

profile of v1, /device:TPU:0, one launch (start us, length us, event | category | flops | bytes accessed | tf_op | source)
XLA Modules:
  0.0 60.3 jit_solution(16454567291798074703)
XLA Ops:
  0.0 0.0 copy-start
  0.0 0.5 collective-permute-start
  0.5 4.1 %collective-permute-start.3 = (bf16[128,1024]{1,0:T(8,128)(2,1)}, bf16[128,1024]{1,0:T(8,128)(2,1)S(1)}, u32[]{:S(2)}, u32[]{:S(2)}) collective-permute-start(bf16[128,1024]{1,0:T(8,128)(2,1)} %param.2), channel_id=1, source_target_pairs={{4,0},{8,4},{12,8},{16,12},{20,16},{24,20},{28,24},{0,28},{5,1},{9... | collective-permute-start | bytes 786440 | tf_op jit(solution)/shard_map/ppermute | solution.py:13
  4.6 0.7 %subtract_bitcast_fusion = s32[8]{0:T(128)S(1)} fusion(s32[1,8]{1,0:T(1,128)} %param.3, s32[]{:T(128)S(6)} %mul.44), kind=kLoop, calls=%fused_computation.69 | loop fusion | flops 8 | bytes 68 | tf_op jit(solution)/shard_map/sub | solution.py:25
  5.2 3.9 %collective-permute-done = bf16[128,1024]{1,0:T(8,128)(2,1)S(1)} collective-permute-done((bf16[128,1024]{1,0:T(8,128)(2,1)}, bf16[128,1024]{1,0:T(8,128)(2,1)S(1)}, u32[]{:S(2)}, u32[]{:S(2)}) %collective-permute-start) | collective-permute-done | bytes 262176 | tf_op jit(solution)/shard_map/ppermute | solution.py:13
  9.1 0.0 collective-permute-start.1
  9.1 1.1 %fusion.56 = f32[8,1024]{1,0:T(8,128)S(1)} fusion(bf16[128,1024]{1,0:T(8,128)(2,1)} %param.2, s32[8]{0:T(128)S(1)} %subtract_bitcast_fusion), kind=kOutput, calls=%fused_computation.67 | convolution fusion | flops 2098176 | bytes 294944 | tf_op jit(solution)/shard_map/dot_general | solution.py:28
  10.3 15.8 %all-gather = f32[64,1024]{1,0:T(8,128)S(1)} all-gather(f32[8,1024]{1,0:T(8,128)S(1)} %fusion.56), channel_id=2, replica_groups=mesh['vec'=8,'rep'=4] {'vec'}, dimensions={0}, use_global_device_ids=true | all-gather | bytes 294912 | tf_op jit(solution)/shard_map/all_gather | solution.py:29
  26.0 0.0 collective-permute-done.3
  26.1 3.2 %collective-permute-start.4 = (bf16[128,1024]{1,0:T(8,128)(2,1)S(1)}, bf16[128,1024]{1,0:T(8,128)(2,1)S(1)}, u32[]{:S(2)}, u32[]{:S(2)}) collective-permute-start(bf16[128,1024]{1,0:T(8,128)(2,1)S(1)} %collective-permute-done.3), channel_id=1, source_target_pairs={{4,0},{8,4},{12,8},{16,12},{20,16},{24,20},{28,24},{0,28},{5,1},{9... | collective-permute-start | bytes 786440 | tf_op jit(solution)/shard_map/ppermute | solution.py:13
  29.2 0.0 collective-permute-done.1
  29.2 0.0 collective-permute-start.2
  29.3 1.0 %convert_element_type.21 = f32[128,1024]{1,0:T(8,128)S(1)} convert(bf16[128,1024]{1,0:T(8,128)(2,1)} %param.2) | non-fusion elementwise | flops 131072 | bytes 786432 | tf_op jit(solution)/shard_map/convert_element_type | solution.py:33
  30.3 0.1 reduce.1
  30.4 0.1 reshape.70
  30.5 3.7 %collective-permute-done.4 = bf16[128,1024]{1,0:T(8,128)(2,1)S(1)} collective-permute-done((bf16[128,1024]{1,0:T(8,128)(2,1)S(1)}, bf16[128,1024]{1,0:T(8,128)(2,1)S(1)}, u32[]{:S(2)}, u32[]{:S(2)}) %collective-permute-start.4) | collective-permute-done | bytes 262176 | tf_op jit(solution)/shard_map/ppermute | solution.py:13
  34.2 3.7 %collective-permute-start.5 = (bf16[128,1024]{1,0:T(8,128)(2,1)S(1)}, bf16[128,1024]{1,0:T(8,128)(2,1)S(1)}, u32[]{:S(2)}, u32[]{:S(2)}) collective-permute-start(bf16[128,1024]{1,0:T(8,128)(2,1)S(1)} %collective-permute-done.4), channel_id=1, source_target_pairs={{4,0},{8,4},{12,8},{16,12},{20,16},{24,20},{28,24},{0,28},{5,1},{9... | collective-permute-start | bytes 786440 | tf_op jit(solution)/shard_map/ppermute | solution.py:13
  37.9 0.0 collective-permute-done.2
  37.9 1.0 %fusion.41 = f32[7,32,128]{2,1,0:T(8,128)S(1)} fusion(bf16[128,1024]{1,0:T(8,128)(2,1)S(1)} %collective-permute-done.2, bf16[128,1024]{1,0:T(8,128)(2,1)} %param.2, s32[]{:T(128)S(6)} %select_n.3), kind=kOutput, calls=%fused_computation.50 | convolution fusion | flops 8388607 | bytes 344068 | tf_op jit(solution)/shard_map/dot_general | solution.py:17
  38.9 1.0 %fusion.40 = f32[7,32,128]{2,1,0:T(8,128)S(1)} fusion(f32[7,32,128]{2,1,0:T(8,128)S(1)} %fusion.41, bf16[128,1024]{1,0:T(8,128)(2,1)S(1)} %collective-permute-done.1, bf16[128,1024]{1,0:T(8,128)(2,1)} %param.2, s32[]{:T(128)S(6)} %select_n.3), kind=kOutput, calls=%fused_computation.48 | convolution fusion | flops 8388608 | bytes 344068 | tf_op jit(solution)/shard_map/dot_general | solution.py:17
  39.9 1.0 %fusion.39 = f32[7,32,128]{2,1,0:T(8,128)S(1)} fusion(f32[7,32,128]{2,1,0:T(8,128)S(1)} %fusion.40, bf16[128,1024]{1,0:T(8,128)(2,1)S(1)} %collective-permute-done, bf16[128,1024]{1,0:T(8,128)(2,1)} %param.2, s32[]{:T(128)S(6)} %select_n.3), kind=kOutput, calls=%fused_computation.46 | convolution fusion | flops 8388608 | bytes 344068 | tf_op jit(solution)/shard_map/dot_general | solution.py:17
  41.0 1.2 %fusion.38 = f32[7,32,128]{2,1,0:T(8,128)S(1)} fusion(f32[7,32,128]{2,1,0:T(8,128)S(1)} %fusion.39, bf16[128,1024]{1,0:T(8,128)(2,1)} %param.2, s32[]{:T(128)S(6)} %select_n.3), kind=kOutput, calls=%fused_computation.44 | convolution fusion | flops 8388608 | bytes 344068 | tf_op jit(solution)/shard_map/dot_general | solution.py:17
  42.2 1.0 %fusion.37 = f32[7,32,128]{2,1,0:T(8,128)S(1)} fusion(f32[7,32,128]{2,1,0:T(8,128)S(1)} %fusion.38, bf16[128,1024]{1,0:T(8,128)(2,1)S(1)} %collective-permute-done.3, bf16[128,1024]{1,0:T(8,128)(2,1)} %param.2, s32[]{:T(128)S(6)} %select_n.3), kind=kOutput, calls=%fused_computation.42 | convolution fusion | flops 8388608 | bytes 344068 | tf_op jit(solution)/shard_map/dot_general | solution.py:17
  43.2 0.0 copy-done
  43.2 0.2 fusion.36
  43.4 0.0 collective-permute-done.5
  43.4 0.2 fusion.35
  43.6 9.8 %all_gather.11 = f32[7,128,128]{2,1,0:T(8,128)S(1)} all-gather(f32[7,32,128]{2,1,0:T(8,128)S(1)} %fusion.35), channel_id=1, replica_groups=mesh['vec'=8,'rep'=4] {'rep'}, dimensions={1}, use_global_device_ids=true | all-gather | bytes 573440 | tf_op jit(solution)/shard_map/all_gather | solution.py:54
  53.4 0.7 %fusion.22 = f32[7,8,128,128]{3,2,1,0:T(8,128)S(1)} fusion(f32[8,1024]{1,0:T(8,128)S(1)} %bitcast_reduce_fusion, f32[128,1024]{1,0:T(8,128)S(1)} %convert_element_type.21, bf16[128,1024]{1,0:T(8,128)(2,1)S(1)} %collective-permute-done.2), kind=kOutput, calls=%fused_computation.24 | convolution fusion | flops 270532608 | bytes 1343488 | tf_op jit(solution)/shard_map/dot_general | solution.py:17
  54.2 0.7 %fusion.24 = f32[7,8,128,128]{3,2,1,0:T(8,128)S(1)} fusion(f32[7,8,128,128]{3,2,1,0:T(8,128)S(1)} %fusion.22, f32[8,1024]{1,0:T(8,128)S(1)} %bitcast_reduce_fusion, f32[128,1024]{1,0:T(8,128)S(1)} %convert_element_type.21, bf16[128,1024]{1,0:T(8,128)(2,1)S(1)} %collective-permute-done.1), kind=kOutput, calls=%fused_computation.26 | convolution fusion | flops 270532608 | bytes 1343488 | tf_op jit(solution)/shard_map/dot_general | solution.py:17
  54.9 0.7 %fusion.26 = f32[7,8,128,128]{3,2,1,0:T(8,128)S(1)} fusion(f32[7,8,128,128]{3,2,1,0:T(8,128)S(1)} %fusion.24, f32[8,1024]{1,0:T(8,128)S(1)} %bitcast_reduce_fusion, f32[128,1024]{1,0:T(8,128)S(1)} %convert_element_type.21, bf16[128,1024]{1,0:T(8,128)(2,1)S(1)} %collective-permute-done), kind=kOutput, calls=%fused_computation.28 | convolution fusion | flops 270532608 | bytes 1343488 | tf_op jit(solution)/shard_map/dot_general | solution.py:17
  55.6 0.7 %fusion.28 = f32[7,8,128,128]{3,2,1,0:T(8,128)S(1)} fusion(f32[7,8,128,128]{3,2,1,0:T(8,128)S(1)} %fusion.26, f32[8,1024]{1,0:T(8,128)S(1)} %bitcast_reduce_fusion, f32[128,1024]{1,0:T(8,128)S(1)} %convert_element_type.21, bf16[128,1024]{1,0:T(8,128)(2,1)S(1)} %copy-done), kind=kOutput, calls=%fused_computation.30 | convolution fusion | flops 270532608 | bytes 1343488 | tf_op jit(solution)/shard_map/dot_general | solution.py:17
  56.3 0.7 %fusion.30 = f32[7,8,128,128]{3,2,1,0:T(8,128)S(1)} fusion(f32[7,8,128,128]{3,2,1,0:T(8,128)S(1)} %fusion.28, f32[8,1024]{1,0:T(8,128)S(1)} %bitcast_reduce_fusion, f32[128,1024]{1,0:T(8,128)S(1)} %convert_element_type.21, bf16[128,1024]{1,0:T(8,128)(2,1)S(1)} %collective-permute-done.3), kind=kOutput, calls=%fused_computation.32 | convolution fusion | flops 270532608 | bytes 1343488 | tf_op jit(solution)/shard_map/dot_general | solution.py:17
  57.0 0.7 %fusion.32 = f32[7,8,128,128]{3,2,1,0:T(8,128)S(1)} fusion(f32[7,8,128,128]{3,2,1,0:T(8,128)S(1)} %fusion.30, f32[8,1024]{1,0:T(8,128)S(1)} %bitcast_reduce_fusion, f32[128,1024]{1,0:T(8,128)S(1)} %convert_element_type.21, bf16[128,1024]{1,0:T(8,128)(2,1)S(1)} %collective-permute-done.4), kind=kOutput, calls=%fused_computation.34 | convolution fusion | flops 270532608 | bytes 1343488 | tf_op jit(solution)/shard_map/dot_general | solution.py:17
  57.7 0.7 %fusion.34 = f32[7,8,128,128]{3,2,1,0:T(8,128)S(1)} fusion(f32[7,8,128,128]{3,2,1,0:T(8,128)S(1)} %fusion.32, f32[8,1024]{1,0:T(8,128)S(1)} %bitcast_reduce_fusion, f32[128,1024]{1,0:T(8,128)S(1)} %convert_element_type.21, bf16[128,1024]{1,0:T(8,128)(2,1)S(1)} %collective-permute-done.5), kind=kOutput, calls=%fused_computation.36 | convolution fusion | flops 270532608 | bytes 1343488 | tf_op jit(solution)/shard_map/dot_general | solution.py:17
  58.4 1.9 %multiply_convert_fusion.8 = bf16[7,8,128,128]{3,2,1,0:T(8,128)(2,1)} fusion(f32[7,8,128,128]{3,2,1,0:T(8,128)S(1)} %fusion.34, f32[7,128,128]{2,1,0:T(8,128)S(1)} %all_gather.11, f32[8]{0:T(128)S(1)} %broadcast_multiply_fusion), kind=kLoop, calls=%fused_computation.8 | loop fusion | flops 3670016 | bytes 5963808 | tf_op jit(solution)/shard_map/convert_element_type | solution.py:58
  (3 shorter events, 0.0 us)
Async XLA Ops:
  0.0 43.2 %copy-start = (bf16[128,1024]{1,0:T(8,128)(2,1)S(1)}, bf16[128,1024]{1,0:T(8,128)(2,1)}, u32[]{:S(2)}) copy-start(bf16[128,1024]{1,0:T(8,128)(2,1)} %param.2) | copy-start | bytes 786436
  0.0 9.1 %collective-permute-start = (bf16[128,1024]{1,0:T(8,128)(2,1)}, bf16[128,1024]{1,0:T(8,128)(2,1)S(1)}, u32[]{:S(2)}, u32[]{:S(2)}) collective-permute-start(bf16[128,1024]{1,0:T(8,128)(2,1)} %param.2), channel_id=1, source_target_pairs={{28,0},{0,4},{4,8},{8,12},{12,16},{16,20},{20,24},{24,28},{29,1},{... | collective-permute-start | bytes 786440 | tf_op jit(solution)/shard_map/ppermute | solution.py:13
  0.5 25.6 %collective-permute-start.3 = (bf16[128,1024]{1,0:T(8,128)(2,1)}, bf16[128,1024]{1,0:T(8,128)(2,1)S(1)}, u32[]{:S(2)}, u32[]{:S(2)}) collective-permute-start(bf16[128,1024]{1,0:T(8,128)(2,1)} %param.2), channel_id=1, source_target_pairs={{4,0},{8,4},{12,8},{16,12},{20,16},{24,20},{28,24},{0,28},{5,1},{9... | collective-permute-start | bytes 786440 | tf_op jit(solution)/shard_map/ppermute | solution.py:13
  9.1 20.1 %collective-permute-start.1 = (bf16[128,1024]{1,0:T(8,128)(2,1)S(1)}, bf16[128,1024]{1,0:T(8,128)(2,1)S(1)}, u32[]{:S(2)}, u32[]{:S(2)}) collective-permute-start(bf16[128,1024]{1,0:T(8,128)(2,1)S(1)} %collective-permute-done), channel_id=1, source_target_pairs={{28,0},{0,4},{4,8},{8,12},{12,16},{16,20},{20,24},{24,28},{29,1},{... | collective-permute-start | bytes 786440 | tf_op jit(solution)/shard_map/ppermute | solution.py:13
  26.1 8.1 %collective-permute-start.4 = (bf16[128,1024]{1,0:T(8,128)(2,1)S(1)}, bf16[128,1024]{1,0:T(8,128)(2,1)S(1)}, u32[]{:S(2)}, u32[]{:S(2)}) collective-permute-start(bf16[128,1024]{1,0:T(8,128)(2,1)S(1)} %collective-permute-done.3), channel_id=1, source_target_pairs={{4,0},{8,4},{12,8},{16,12},{20,16},{24,20},{28,24},{0,28},{5,1},{9... | collective-permute-start | bytes 786440 | tf_op jit(solution)/shard_map/ppermute | solution.py:13
  29.2 8.6 %collective-permute-start.2 = (bf16[128,1024]{1,0:T(8,128)(2,1)S(1)}, bf16[128,1024]{1,0:T(8,128)(2,1)S(1)}, u32[]{:S(2)}, u32[]{:S(2)}) collective-permute-start(bf16[128,1024]{1,0:T(8,128)(2,1)S(1)} %collective-permute-done.1), channel_id=1, source_target_pairs={{28,0},{0,4},{4,8},{8,12},{12,16},{16,20},{20,24},{24,28},{29,1},{... | collective-permute-start | bytes 786440 | tf_op jit(solution)/shard_map/ppermute | solution.py:13
  34.2 9.3 %collective-permute-start.5 = (bf16[128,1024]{1,0:T(8,128)(2,1)S(1)}, bf16[128,1024]{1,0:T(8,128)(2,1)S(1)}, u32[]{:S(2)}, u32[]{:S(2)}) collective-permute-start(bf16[128,1024]{1,0:T(8,128)(2,1)S(1)} %collective-permute-done.4), channel_id=1, source_target_pairs={{4,0},{8,4},{12,8},{16,12},{20,16},{24,20},{28,24},{0,28},{5,1},{9... | collective-permute-start | bytes 786440 | tf_op jit(solution)/shard_map/ppermute | solution.py:13
